TPU v7x, 32 devices: a whole 2x2x4 slice. The times are simulated.
32 devices in a mesh: rep: 16 (over z, y, core), fsdp: 2 (over x).
Axes of the slice: x: 2, y: 2, z: 4, core: 2. Of those that a mesh axis runs over, the one named last changes fastest.
Arguments:
- tokens: bfloat16 [256, 197, 384], P(('rep', 'fsdp')), may hold values from -6 to 6
- gain_one: bfloat16 [384], P('fsdp'), may hold values from 0.25 to 1.75
- shift_one: bfloat16 [384], P('fsdp'), may hold values from -1.75 to 1.75
- qkv_weight: bfloat16 [384, 1152], P('fsdp'), may hold values from -0.3125 to 0.3125
- query_bias: bfloat16 [384], P('fsdp'), may hold values from -3 to 3
- value_bias: bfloat16 [384], P('fsdp'), may hold values from -3 to 3
- out_weight: bfloat16 [384, 384], P('fsdp'), may hold values from -1.25 to 1.25
- out_bias: bfloat16 [384], P('fsdp'), may hold values from -1.75 to 1.75
- gain_two: bfloat16 [384], P('fsdp'), may hold values from 0.25 to 1.75
- shift_two: bfloat16 [384], P('fsdp'), may hold values from -1.75 to 1.75
- lift_weight: bfloat16 [384, 1536], P('fsdp'), may hold values from -0.3125 to 0.3125
- lift_bias: bfloat16 [1536], P('fsdp'), may hold values from -3 to 3
- drop_weight: bfloat16 [1536, 384], P('fsdp'), may hold values from -0.15625 to 0.15625
- drop_bias: bfloat16 [384], P('fsdp'), may hold values from -1.75 to 1.75
- cotangent: bfloat16 [256, 197, 384], P(('rep', 'fsdp')), may hold values from -12 to 12
Outputs:
- output: bfloat16 [256, 197, 384], P(('rep', 'fsdp'))
- input_grad: bfloat16 [256, 197, 384], P(('rep', 'fsdp'))
- grad_gain_one: float32 [384], P('fsdp')
- grad_shift_one: float32 [384], P('fsdp')
- grad_qkv_weight: float32 [384, 1152], P('fsdp')
- grad_query_bias: float32 [384], P('fsdp')
- grad_value_bias: float32 [384], P('fsdp')
- grad_out_weight: float32 [384, 384], P('fsdp')
- grad_out_bias: float32 [384], P('fsdp')
- grad_gain_two: float32 [384], P('fsdp')
- grad_shift_two: float32 [384], P('fsdp')
- grad_lift_weight: float32 [384, 1536], P('fsdp')
- grad_lift_bias: float32 [1536], P('fsdp')
- grad_drop_weight: float32 [1536, 384], P('fsdp')
- grad_drop_bias: float32 [384], P('fsdp')
All inputs are finite; a program needn't handle non-finite values.
Results may differ from a plain program's by a relative error of at most 0.023.
Values may be sent and summed in bfloat16 or wider, within the bound.
No kernel may reach another device: no remote copies, remote signals or barrier semaphores. Data moves between devices by JAX's collectives and lax.ppermute only.
A program may use at most 128 MiB of HBM per device.

v0:
```python
import jax
import jax.numpy as jnp
from jax import lax
from jax.sharding import PartitionSpec as P

HEADS = 6
HEAD_DIM = 64
epsilon = 1e-06
root_half = 0.7071067811865476
gauss_norm = 0.3989422804014327


def norm_forward(inputs, gain_vec, shift_vec):
    average = jnp.mean(inputs, axis=-1, keepdims=True)
    centred = inputs - average
    variance = jnp.mean(centred * centred, axis=-1, keepdims=True)
    inverse = lax.rsqrt(variance + epsilon)
    normal = centred * inverse
    return (normal * gain_vec + shift_vec, normal, inverse)


def norm_backward(grad_out, normal, inverse, gain_vec):
    grad_gain = jnp.sum(grad_out * normal, axis=0)
    grad_shift = jnp.sum(grad_out, axis=0)
    scaled = grad_out * gain_vec
    grad_in = inverse * (
        scaled
        - jnp.mean(scaled, axis=-1, keepdims=True)
        - normal * jnp.mean(scaled * normal, axis=-1, keepdims=True)
    )
    return (grad_in, grad_gain, grad_shift)


def product(left, right):
    return jnp.dot(left, right, preferred_element_type=jnp.float32)


def product_left(left, right):
    return lax.dot_general(
        left, right, (((0,), (0,)), ((), ())), preferred_element_type=jnp.float32
    )


def product_right(left, right):
    return lax.dot_general(
        left, right, (((1,), (1,)), ((), ())), preferred_element_type=jnp.float32
    )


def raw_scores(query_part, key_part):
    scale_factor = query_part.shape[-1] ** (-0.5)
    return (
        jnp.einsum("iqhe,ikhe->ihqk", query_part, key_part, preferred_element_type=jnp.float32)
        * scale_factor
    )


def per_device(
    tokens,
    gain_one,
    shift_one,
    qkv_weight,
    query_bias,
    value_bias,
    out_weight,
    out_bias,
    gain_two,
    shift_two,
    lift_weight,
    lift_bias,
    drop_weight,
    drop_bias,
    cotangent,
):
    gathered = (
        lax.all_gather(gain_one, "fsdp", axis=0, tiled=True),
        lax.all_gather(shift_one, "fsdp", axis=0, tiled=True),
        lax.all_gather(qkv_weight, "fsdp", axis=0, tiled=True),
        lax.all_gather(query_bias, "fsdp", axis=0, tiled=True),
        lax.all_gather(value_bias, "fsdp", axis=0, tiled=True),
        lax.all_gather(out_weight, "fsdp", axis=0, tiled=True),
        lax.all_gather(out_bias, "fsdp", axis=0, tiled=True),
        lax.all_gather(gain_two, "fsdp", axis=0, tiled=True),
        lax.all_gather(shift_two, "fsdp", axis=0, tiled=True),
        lax.all_gather(lift_weight, "fsdp", axis=0, tiled=True),
        lax.all_gather(lift_bias, "fsdp", axis=0, tiled=True),
        lax.all_gather(drop_weight, "fsdp", axis=0, tiled=True),
        lax.all_gather(drop_bias, "fsdp", axis=0, tiled=True),
    )
    (
        full_gain_one,
        full_shift_one,
        full_qkv,
        full_query_bias,
        full_value_bias,
        full_out,
        full_out_bias,
        full_gain_two,
        full_shift_two,
        full_lift,
        full_lift_bias,
        full_drop,
        full_drop_bias,
    ) = gathered
    images, length, width = tokens.shape
    tok_rows = images * length
    scale_factor = HEAD_DIM ** (-0.5)
    flat_in = tokens.astype(jnp.float32).reshape(tok_rows, width)
    normed_f, normal_one, inverse_one = norm_forward(
        flat_in, full_gain_one.astype(jnp.float32), full_shift_one.astype(jnp.float32)
    )
    normed = normed_f.astype(jnp.bfloat16)
    qkv_bias = jnp.concatenate(
        [full_query_bias, jnp.zeros_like(full_query_bias), full_value_bias]
    ).astype(jnp.float32)
    projected = (product(normed, full_qkv) + qkv_bias).astype(jnp.bfloat16)
    split_heads = projected.reshape(images, length, 3, HEADS, HEAD_DIM)
    query_part = split_heads[:, :, 0]
    key_part = split_heads[:, :, 1]
    value_part = split_heads[:, :, 2]
    scores = raw_scores(query_part, key_part)
    top_score = jnp.max(scores, axis=-1, keepdims=True)
    log_total = top_score + jnp.log(jnp.sum(jnp.exp(scores - top_score), axis=-1, keepdims=True))
    soft_weights = jnp.exp(scores - log_total).astype(jnp.bfloat16)
    mixed = (
        jnp.einsum("ihqk,ikhe->iqhe", soft_weights, value_part, preferred_element_type=jnp.float32)
        .reshape(tok_rows, width)
        .astype(jnp.bfloat16)
    )
    middle = flat_in + product(mixed, full_out) + full_out_bias.astype(jnp.float32)
    normed_two_f, normal_two, inverse_two = norm_forward(
        middle, full_gain_two.astype(jnp.float32), full_shift_two.astype(jnp.float32)
    )
    normed_two = normed_two_f.astype(jnp.bfloat16)
    hidden = product(normed_two, full_lift) + full_lift_bias.astype(jnp.float32)
    active = jax.nn.gelu(hidden, approximate=False).astype(jnp.bfloat16)
    result = middle + product(active, full_drop) + full_drop_bias.astype(jnp.float32)
    output = result.astype(jnp.bfloat16).reshape(tokens.shape)
    back_gain_one, back_qkv, back_out, back_gain_two, back_lift, back_drop = (
        lax.all_gather(gain_one, "fsdp", axis=0, tiled=True),
        lax.all_gather(qkv_weight, "fsdp", axis=0, tiled=True),
        lax.all_gather(out_weight, "fsdp", axis=0, tiled=True),
        lax.all_gather(gain_two, "fsdp", axis=0, tiled=True),
        lax.all_gather(lift_weight, "fsdp", axis=0, tiled=True),
        lax.all_gather(drop_weight, "fsdp", axis=0, tiled=True),
    )
    grad_flat = cotangent.reshape(tok_rows, width)
    grad_outer = grad_flat.astype(jnp.float32)
    grad_drop_weight = product_left(active, grad_flat)
    grad_drop_bias = jnp.sum(grad_outer, axis=0)
    d_active = product_right(grad_flat, back_drop)
    slope = (
        0.5 * (1.0 + lax.erf(hidden * root_half))
        + hidden * jnp.exp(-0.5 * hidden * hidden) * gauss_norm
    )
    d_hidden = (d_active * slope).astype(jnp.bfloat16)
    grad_lift_weight = product_left(normed_two, d_hidden)
    grad_lift_bias = jnp.sum(d_hidden.astype(jnp.float32), axis=0)
    d_normed_two = product_right(d_hidden, back_lift)
    d_from_norm, grad_gain_two, grad_shift_two = norm_backward(
        d_normed_two, normal_two, inverse_two, back_gain_two.astype(jnp.float32)
    )
    d_middle = grad_outer + d_from_norm
    d_attended = d_middle.astype(jnp.bfloat16)
    grad_out_weight = product_left(mixed, d_attended)
    grad_out_bias = jnp.sum(d_attended.astype(jnp.float32), axis=0)
    d_mixed = (
        product_right(d_attended, back_out)
        .astype(jnp.bfloat16)
        .reshape(images, length, HEADS, HEAD_DIM)
    )
    again_probs = jnp.exp(raw_scores(query_part, key_part) - log_total)
    again_soft = again_probs.astype(jnp.bfloat16)
    d_value = jnp.einsum("ihqk,iqhe->ikhe", again_soft, d_mixed, preferred_element_type=jnp.float32)
    d_probs = jnp.einsum("iqhe,ikhe->ihqk", d_mixed, value_part, preferred_element_type=jnp.float32)
    row_delta = jnp.sum(again_probs * d_probs, axis=-1, keepdims=True)
    d_scores = (again_probs * (d_probs - row_delta)).astype(jnp.bfloat16)
    d_query = (
        jnp.einsum("ihqk,ikhe->iqhe", d_scores, key_part, preferred_element_type=jnp.float32)
        * scale_factor
    )
    d_key = (
        jnp.einsum("ihqk,iqhe->ikhe", d_scores, query_part, preferred_element_type=jnp.float32)
        * scale_factor
    )
    d_projected = (
        jnp.stack([d_query, d_key, d_value], axis=2)
        .reshape(tok_rows, 3 * width)
        .astype(jnp.bfloat16)
    )
    grad_qkv_weight = product_left(normed, d_projected)
    column_sums = jnp.sum(d_projected.astype(jnp.float32), axis=0)
    grad_query_bias = column_sums[:width]
    grad_value_bias = column_sums[2 * width :]
    d_normed = product_right(d_projected, back_qkv)
    d_first, grad_gain_one, grad_shift_one = norm_backward(
        d_normed, normal_one, inverse_one, back_gain_one.astype(jnp.float32)
    )
    input_grad = (d_middle + d_first).astype(jnp.bfloat16).reshape(tokens.shape)
    owned = (
        lax.psum_scatter(
            grad_gain_one.astype(jnp.bfloat16), "fsdp", scatter_dimension=0, tiled=True
        ).astype(jnp.float32),
        lax.psum_scatter(
            grad_shift_one.astype(jnp.bfloat16), "fsdp", scatter_dimension=0, tiled=True
        ).astype(jnp.float32),
        lax.psum_scatter(
            grad_qkv_weight.astype(jnp.bfloat16), "fsdp", scatter_dimension=0, tiled=True
        ).astype(jnp.float32),
        lax.psum_scatter(
            grad_query_bias.astype(jnp.bfloat16), "fsdp", scatter_dimension=0, tiled=True
        ).astype(jnp.float32),
        lax.psum_scatter(
            grad_value_bias.astype(jnp.bfloat16), "fsdp", scatter_dimension=0, tiled=True
        ).astype(jnp.float32),
        lax.psum_scatter(
            grad_out_weight.astype(jnp.bfloat16), "fsdp", scatter_dimension=0, tiled=True
        ).astype(jnp.float32),
        lax.psum_scatter(
            grad_out_bias.astype(jnp.bfloat16), "fsdp", scatter_dimension=0, tiled=True
        ).astype(jnp.float32),
        lax.psum_scatter(
            grad_gain_two.astype(jnp.bfloat16), "fsdp", scatter_dimension=0, tiled=True
        ).astype(jnp.float32),
        lax.psum_scatter(
            grad_shift_two.astype(jnp.bfloat16), "fsdp", scatter_dimension=0, tiled=True
        ).astype(jnp.float32),
        lax.psum_scatter(
            grad_lift_weight.astype(jnp.bfloat16), "fsdp", scatter_dimension=0, tiled=True
        ).astype(jnp.float32),
        lax.psum_scatter(
            grad_lift_bias.astype(jnp.bfloat16), "fsdp", scatter_dimension=0, tiled=True
        ).astype(jnp.float32),
        lax.psum_scatter(
            grad_drop_weight.astype(jnp.bfloat16), "fsdp", scatter_dimension=0, tiled=True
        ).astype(jnp.float32),
        lax.psum_scatter(
            grad_drop_bias.astype(jnp.bfloat16), "fsdp", scatter_dimension=0, tiled=True
        ).astype(jnp.float32),
    )
    final = (
        lax.psum(owned[0].astype(jnp.bfloat16), "rep").astype(jnp.float32),
        lax.psum(owned[1].astype(jnp.bfloat16), "rep").astype(jnp.float32),
        lax.psum(owned[2].astype(jnp.bfloat16), "rep").astype(jnp.float32),
        lax.psum(owned[3].astype(jnp.bfloat16), "rep").astype(jnp.float32),
        lax.psum(owned[4].astype(jnp.bfloat16), "rep").astype(jnp.float32),
        lax.psum(owned[5].astype(jnp.bfloat16), "rep").astype(jnp.float32),
        lax.psum(owned[6].astype(jnp.bfloat16), "rep").astype(jnp.float32),
        lax.psum(owned[7].astype(jnp.bfloat16), "rep").astype(jnp.float32),
        lax.psum(owned[8].astype(jnp.bfloat16), "rep").astype(jnp.float32),
        lax.psum(owned[9].astype(jnp.bfloat16), "rep").astype(jnp.float32),
        lax.psum(owned[10].astype(jnp.bfloat16), "rep").astype(jnp.float32),
        lax.psum(owned[11].astype(jnp.bfloat16), "rep").astype(jnp.float32),
        lax.psum(owned[12].astype(jnp.bfloat16), "rep").astype(jnp.float32),
    )
    return (output, input_grad) + tuple(final)


def solution(mesh):
    in_specs = (
        P(("rep", "fsdp"), None, None),
        P("fsdp"),
        P("fsdp"),
        P("fsdp", None),
        P("fsdp"),
        P("fsdp"),
        P("fsdp", None),
        P("fsdp"),
        P("fsdp"),
        P("fsdp"),
        P("fsdp", None),
        P("fsdp"),
        P("fsdp", None),
        P("fsdp"),
        P(("rep", "fsdp"), None, None),
    )
    out_specs = (
        P(("rep", "fsdp"), None, None),
        P(("rep", "fsdp"), None, None),
        P("fsdp"),
        P("fsdp"),
        P("fsdp", None),
        P("fsdp"),
        P("fsdp"),
        P("fsdp", None),
        P("fsdp"),
        P("fsdp"),
        P("fsdp"),
        P("fsdp", None),
        P("fsdp"),
        P("fsdp", None),
        P("fsdp"),
    )
    return jax.shard_map(
        per_device, mesh=mesh, in_specs=in_specs, out_specs=out_specs, check_vma=False
    )
```

profile of v0, /device:TPU:0, one launch (start us, length us, event | category | flops | bytes accessed | tf_op | source)
XLA Modules:
  0.0 416.0 jit_solution(2073940774700629270)
XLA Ops:
  16.4 5.9 %all-reduce.20 = (bf16[384]{0:T(512)(128)(2,1)S(1)}, bf16[384]{0:T(512)(128)(2,1)S(1)}, bf16[384]{0:T(512)(128)(2,1)S(1)}, bf16[384]{0:T(512)(128)(2,1)S(1)}, bf...) all-reduce(bf16[384]{0:T(512)(128)(2,1)S(1)} %dynamic-update-slice., ...), channel_id=1, replica_groups=mesh['rep'=16,'fsdp'=2] {'fsdp'}, use_global_device_ids=true, to_apply=%add.3 | all-reduce | flops 2688 | bytes 10752
  22.3 2.0 reshape.179
  24.4 20.0 %all_gather.47 = bf16[384,1152]{1,0:T(8,128)(2,1)S(1)} all-gather(bf16[192,1152]{1,0:T(8,128)(2,1)S(1)} %copy-done.15), channel_id=1, replica_groups=mesh['rep'=16,'fsdp'=2] {'fsdp'}, dimensions={0}, use_global_device_ids=true | all-gather | bytes 1327104 | tf_op jit(solution)/shard_map/all_gather | solution.py:78
  45.3 4.2 %fusion.16 = bf16[1576,1152]{1,0:T(8,128)(2,1)} fusion(bf16[384,1152]{1,0:T(8,128)(2,1)S(1)} %all_gather.47, f32[1152]{0:T(1024)S(1)} %maximum_convert_fusion.1, f32[1576,384]{1,0:T(8,128)S(1)} %reshape.179, f32[384]{0:T(512)S(1)} %convert_element_type.206, f32[384]{0:T(512)S(1)} %convert_element_type.205, f32[1576]{0:T(1024)S(1)} %rsqrt.21, f32[1576]{0:T(1024)S(1)} %div.27), kind=kOutput, calls=%fused_computation.34 | convolution fusion | flops 1401000960 | bytes 6956864 | tf_op jit(solution)/shard_map/dot_general | solution.py:35
  49.5 11.8 %reshape.237 = bf16[8,197,3,6,64]{4,3,2,1,0:T(8,128)(2,1)} reshape(bf16[1576,1152]{1,0:T(8,128)(2,1)} %fusion.16) | data formatting | bytes 7262208 | tf_op jit(solution)/shard_map/reshape | solution.py:117
  61.2 6.7 %fusion.43 = (bf16[8,197,1,6,64]{4,3,2,1,0:T(8,128)(2,1)}, bf16[8,197,1,6,64]{4,3,2,1,0:T(8,128)(2,1)}, bf16[8,197,1,6,64]{4,3,2,1,0:T(8,128)(2,1)}) fusion(bf16[8,197,3,6,64]{4,3,2,1,0:T(8,128)(2,1)} %reshape.237), kind=kLoop, calls=%fused_computation.96 | loop fusion | bytes 7262208 | tf_op jit(solution)/shard_map/slice | solution.py:118
  67.9 3.5 copy.114
  71.4 4.0 copy.115
  77.0 2.0 exponential_reduce_fusion
  80.8 3.5 copy.113
  84.3 6.3 %fusion.29 = bf16[8,197,6,64]{1,3,2,0:T(8,128)(2,1)S(1)} fusion(bf16[8,197,1,6,64]{1,4,3,0,2:T(8,128)(2,1)S(1)} %copy.113, f32[8,6,197,197]{2,3,1,0:T(8,128)} %copy-done, f32[8,6,197]{2,1,0:T(8,128)S(1)} %log_add_fusion), kind=kOutput, calls=%fused_computation.73 | convolution fusion | flops 244636176 | bytes 9909888 | tf_op jit(solution)/shard_map/ihqk,ikhe->iqhe/dot_general | solution.py:126
  91.6 2.6 convert_element_type.213
  94.2 6.2 %all_gather.50 = bf16[384,384]{1,0:T(8,128)(2,1)S(1)} all-gather(bf16[192,384]{1,0:T(8,128)(2,1)S(1)} %copy-done.17), channel_id=1, replica_groups=mesh['rep'=16,'fsdp'=2] {'fsdp'}, dimensions={0}, use_global_device_ids=true | all-gather | bytes 442368 | tf_op jit(solution)/shard_map/all_gather | solution.py:81
  100.4 3.2 fusion.46
  104.3 4.3 %all-gather = bf16[2,1,768]{2,1,0:T(2,128)(2,1)S(1)} all-gather(bf16[1,1,768]{2,1,0:T(2,128)(2,1)S(1)} %reshape.209), channel_id=1, replica_groups=mesh['rep'=16,'fsdp'=2] {'fsdp'}, dimensions={0}, use_global_device_ids=true | all-gather | bytes 4608 | tf_op jit(solution)/shard_map/all_gather | solution.py:86
  108.7 2.5 copy.93
  111.2 2.7 reshape.182
  117.0 2.7 convert_element_type.235
  119.7 26.4 %fusion.2 = (bf16[1576,1536]{1,0:T(8,128)(2,1)}, f32[1576,1536]{1,0:T(8,128)}) fusion(f32[1536]{0:T(1024)S(1)} %reshape.211, bf16[384,1536]{1,0:T(8,128)(2,1)} %all-gather.4.cloned.1.call-done, f32[1576,384]{1,0:T(8,128)S(1)} %get-tuple-element.127, f32[384]{0:T(512)S(1)} %convert_element_type.216, f32[384]{0:T(512)S(1)} %convert_element_type.215, ...), kind=kOutput, calls=%fused_computation.9 | convolution fusion | flops 2021919744 | bytes 18146624 | tf_op jit(solution)/shard_map/dot_general | solution.py:35
  146.0 8.6 %fusion.47 = (bf16[1536]{0:T(1024)(128)(2,1)S(1)}, bf16[1576,1536]{1,0:T(8,128)(2,1)S(1)}) fusion(f32[1576,1536]{1,0:T(8,128)} %get-tuple-element.129, bf16[1576,384]{1,0:T(8,128)(2,1)} %reshape.182, bf16[1536,384]{1,0:T(8,128)(2,1)} %all-gather.6.cloned.1.call-done), kind=kOutput, calls=%fused_computation.100 | convolution fusion | flops 1885751808 | bytes 16917504 | tf_op jit(solution)/shard_map/dot_general | solution.py:45
  154.7 3.3 multiply_reduce_fusion.2
  158.0 3.2 convert_reduce_fusion.2
  162.8 2.1 convolution_convert_fusion.3
  164.9 4.8 %reshape.238 = bf16[8,197,6,64]{3,2,1,0:T(8,128)(2,1)} reshape(bf16[1576,384]{1,0:T(8,128)(2,1)} %convolution_convert_fusion.3) | data formatting | bytes 2420736 | tf_op jit(solution)/shard_map/reshape | solution.py:170
  169.6 5.0 %copy.95 = bf16[8,197,6,64]{1,3,2,0:T(8,128)(2,1)} copy(bf16[8,197,6,64]{3,2,1,0:T(8,128)(2,1)} %reshape.238) | data formatting | bytes 2420736 | tf_op jit(solution)/shard_map/reshape | solution.py:170
  174.6 11.1 %multiply_reduce_fusion = (f32[8,6,197]{2,1,0:T(8,128)S(1)}, f32[8,6,197,197]{2,3,1,0:T(8,128)}) fusion(f32[8,6,197,197]{2,3,1,0:T(8,128)} %copy-done, f32[8,6,197]{2,1,0:T(8,128)S(1)} %log_add_fusion, bf16[8,197,6,64]{1,3,2,0:T(8,128)(2,1)} %copy.95, bf16[8,197,1,6,64]{1,4,3,0,2:T(8,128)(2,1)} %copy-done.7), kind=kOutput, calls=%fused_computation.3 | convolution fusion | flops 245884368 | bytes 17399040 | tf_op jit(solution)/shard_map/iqhe,ikhe->ihqk/dot_general | solution.py:175
  185.7 11.5 %multiply_convert_fusion = bf16[8,6,197,197]{2,3,1,0:T(8,128)(2,1)} fusion(f32[8,6,197,197]{2,3,1,0:T(8,128)} %get-tuple-element.132, f32[8,6,197,197]{2,3,1,0:T(8,128)} %copy-done, f32[8,6,197]{2,1,0:T(8,128)S(1)} %get-tuple-element.131, f32[8,6,197]{2,1,0:T(8,128)S(1)} %log_add_fusion), kind=kLoop, calls=%fused_computation.2 | loop fusion | flops 9314160 | bytes 18703968 | tf_op jit(solution)/shard_map/convert_element_type | solution.py:177
  197.2 5.2 %multiply_bitcast_fusion.1 = bf16[8,197,1,6,64]{1,4,3,0,2:T(8,128)(2,1)} fusion(bf16[8,6,197,197]{2,3,1,0:T(8,128)(2,1)} %multiply_convert_fusion, bf16[8,197,1,6,64]{1,4,3,0,2:T(8,128)(2,1)} %copy-done.1), kind=kOutput, calls=%fused_computation.37 | convolution fusion | flops 239652864 | bytes 6146400 | tf_op jit(solution)/shard_map/ihqk,ikhe->iqhe/dot_general | solution.py:179
  202.4 5.4 %multiply_bitcast_fusion = bf16[8,197,1,6,64]{1,4,3,0,2:T(8,128)(2,1)} fusion(bf16[8,6,197,197]{2,3,1,0:T(8,128)(2,1)} %multiply_convert_fusion, bf16[8,197,1,6,64]{1,4,3,0,2:T(8,128)(2,1)S(1)} %copy-done.10), kind=kOutput, calls=%fused_computation.36 | convolution fusion | flops 239652864 | bytes 6146400 | tf_op jit(solution)/shard_map/ihqk,iqhe->ikhe/dot_general | solution.py:183
  207.9 3.1 convolution_bitcast_fusion
  211.0 3.2 fusion.42
  214.2 5.5 %copy.100 = bf16[8,197,3,6,64]{1,0,4,3,2:T(8,128)(2,1)} copy(bf16[8,197,3,6,64]{1,4,3,0,2:T(8,128)(2,1)S(1)} %get-tuple-element.116) | data formatting | bytes 7262208 | tf_op jit(solution)/shard_map/convert_element_type | solution.py:189
  219.6 8.9 %convert_element_type.228 = bf16[1576,1152]{0,1:T(8,128)(2,1)} reshape(bf16[8,197,3,6,64]{1,0,4,3,2:T(8,128)(2,1)} %copy.100) | data formatting | bytes 7262208 | tf_op jit(solution)/shard_map/convert_element_type | solution.py:189
  228.5 5.4 %convolution_convert_fusion = bf16[384,1152]{1,0:T(8,128)(2,1)} fusion(bf16[1576,384]{1,0:T(8,128)(2,1)} %convert_element_type.235, bf16[1576,1152]{0,1:T(8,128)(2,1)} %convert_element_type.228), kind=kOutput, calls=%fused_computation.42 | convolution fusion | flops 1394786304 | bytes 5726208 | tf_op jit(solution)/shard_map/dot_general | solution.py:39
  233.9 6.6 %convolution_convert_fusion.2 = bf16[384,1536]{1,0:T(8,128)(2,1)} fusion(bf16[1576,1536]{1,0:T(8,128)(2,1)} %copy-done.37, f32[1576,384]{1,0:T(8,128)} %copy-done.2, f32[384]{0:T(512)S(1)} %convert_element_type.216, f32[384]{0:T(512)S(1)} %convert_element_type.215, f32[1576]{0:T(1024)S(1)} %add_rsqrt_fusion, f32[1576]{0:T(1024)S(1)} %broadcast_multiply_fusion.4), kind=kOutput, calls=%fused_computation.45 | convolution fusion | flops 1862740992 | bytes 8457536 | tf_op jit(solution)/shard_map/dot_general | solution.py:39
  240.7 6.8 %convolution_convert_fusion.1 = bf16[1536,384]{1,0:T(8,128)(2,1)} fusion(bf16[1576,1536]{1,0:T(8,128)(2,1)} %get-tuple-element.128, bf16[1576,384]{1,0:T(8,128)(2,1)} %reshape.182), kind=kOutput, calls=%fused_computation.44 | convolution fusion | flops 1859715072 | bytes 7231488 | tf_op jit(solution)/shard_map/dot_general | solution.py:39
  250.9 6.4 %multiply_reduce_fusion.3 = (bf16[384]{0:T(512)(128)(2,1)S(1)}, f32[1576]{0:T(1024)S(1)}, f32[1576]{0:T(1024)S(1)}, bf16[384]{0:T(512)(128)(2,1)S(1)}, f32[1576,384]{1,0:T(8,128)S(1)}) fusion(f32[1576,384]{1,0:T(8,128)} %copy-done.4, f32[1576]{0:T(1024)S(1)} %copy-done.22, f32[1576]{0:T(1024)S(1)} %copy-done.20, f32[384]{0:T(512)S(1)} %copy-done.24, ...), kind=kOutput, calls=%fused_computation.49 | convolution fusion | flops 1399786752 | bytes 9385600 | tf_op jit(solution)/shard_map/dot_general | solution.py:45
  257.4 2.2 add_convert_fusion.1
  259.6 17.5 %reduce-scatter.9.cloned.1.call-done = bf16[192,1536]{1,0:T(8,128)(2,1)} async-done(((bf16[384,1536]{1,0:T(8,128)(2,1)}), bf16[192,1536]{1,0:T(8,128)(2,1)}) %reduce-scatter.9.cloned.1.call-update) | async-done | bytes 589840 | tf_op jit(solution)/shard_map/reduce_scatter | solution.py:228
  277.1 24.5 %reduce-scatter.11.cloned.1.call-done = bf16[768,384]{1,0:T(8,128)(2,1)} async-done(((bf16[1536,384]{1,0:T(8,128)(2,1)}), bf16[768,384]{1,0:T(8,128)(2,1)}) %reduce-scatter.11.cloned.1.call-update) | async-done | bytes 589840 | tf_op jit(solution)/shard_map/reduce_scatter | solution.py:234
  301.8 7.0 %all-reduce.19 = (bf16[384]{0:T(512)(128)(2,1)S(1)}, bf16[384]{0:T(512)(128)(2,1)S(1)}, bf16[384]{0:T(512)(128)(2,1)S(1)}, bf16[384]{0:T(512)(128)(2,1)S(1)}, bf...) all-reduce(bf16[384]{0:T(512)(128)(2,1)S(1)} %dynamic-update-slice., ...), channel_id=1, replica_groups=mesh['rep'=16,'fsdp'=2] {'fsdp'}, use_global_device_ids=true, to_apply=%add.7 | all-reduce | flops 4992 | bytes 19968
  309.5 32.4 %all-reduce.17 = (bf16[192]{0:T(256)(128)(2,1)S(1)}, bf16[192]{0:T(256)(128)(2,1)S(1)}, bf16[192]{0:T(256)(128)(2,1)S(1)}, bf16[192]{0:T(256)(128)(2,1)S(1)}, bf...) all-reduce(bf16[192]{0:T(256)(128)(2,1)S(1)} %dynamic-slice.9, ...), channel_id=1, replica_groups=mesh['rep'=16,'fsdp'=2] {'rep'}, use_global_device_ids=true, to_apply=%region_13.0 | all-reduce | flops 2304 | bytes 9216 | tf_op jit(solution)/shard_map/psum | solution.py:242
  347.0 2.9 reshape.184
  349.9 2.6 copy.104
  352.4 6.1 %fusion.20 = bf16[1576,384]{1,0:T(8,128)(2,1)} fusion(f32[1576,384]{1,0:T(8,128)S(1)} %copy-done.3, bf16[1576,1536]{1,0:T(8,128)(2,1)} %get-tuple-element.128, bf16[1536,384]{1,0:T(8,128)(2,1)S(1)} %copy-done.27, f32[384]{0:T(512)S(1)} %convert_element_type.220), kind=kOutput, calls=%fused_computation.43 | convolution fusion | flops 1860940800 | bytes 9653760 | tf_op jit(solution)/shard_map/dot_general | solution.py:35
  361.4 41.4 %all-reduce.23.cloned.1.call-done = (bf16[192,1152]{1,0:T(8,128)(2,1)}, bf16[192,384]{1,0:T(8,128)(2,1)}, bf16[192,1536]{1,0:T(8,128)(2,1)}, bf16[768,384]{1,0:T(8,128)(2,1)}) async-done(((bf16[192,1152]{1,0:T(8,128)(2,1)}, bf16[192,384]{1,0:T(8,128)(2,1)}, bf16[192,1536]{1,0:T(8,128)(2,1)}, bf16[768,384]{1,0:T(8,128)(2,1)}), (bf16[192,1152]{1,0:T(8,128)(2,1)}, bf16[192,384]{1,0:T(8,128)(2,1)}, ...) | async-done | bytes 1769488 | tf_op jit(solution)/shard_map/psum | solution.py:244
  402.8 2.3 convert_element_type.251
  405.1 2.2 convert_element_type.254
  (178 shorter events, 31.7 us)
Async XLA Ops:
  7.2 3.1 copy-start.6
  7.2 112.5 %all-gather.4.cloned.1.call-start = ((), (), s32[]{:S(2)}) async-start(), calls=%async_computation.4 | async-start | bytes 1769472 | tf_op jit(solution)/shard_map/all_gather | solution.py:85
  7.9 138.1 %all-gather.6.cloned.1.call-start = ((), (), s32[]{:S(2)}) async-start(), calls=%async_computation.5 | async-start | bytes 1769472 | tf_op jit(solution)/shard_map/all_gather | solution.py:87
  8.7 250.9 %reduce-scatter.7.cloned.1.call-start = ((), (), s32[]{:S(2)}) async-start(), calls=%async_computation.7 | async-start | bytes 442368 | tf_op jit(solution)/shard_map/reduce_scatter | solution.py:216
  10.3 3.0 copy-start.25
  10.3 4.3 %copy-start.29 = (bf16[192]{0:T(256)(128)(2,1)S(1)}, bf16[192]{0:T(256)(128)(2,1)}, u32[]{:S(2)}) copy-start(bf16[192]{0:T(256)(128)(2,1)} %param.16) | copy-start | bytes 1156
  10.3 4.5 %copy-start.30 = (bf16[192]{0:T(256)(128)(2,1)S(1)}, bf16[192]{0:T(256)(128)(2,1)}, u32[]{:S(2)}) copy-start(bf16[192]{0:T(256)(128)(2,1)} %param.17) | copy-start | bytes 1156
  10.4 4.8 %copy-start.31 = (bf16[192]{0:T(256)(128)(2,1)S(1)}, bf16[192]{0:T(256)(128)(2,1)}, u32[]{:S(2)}) copy-start(bf16[192]{0:T(256)(128)(2,1)} %param.19) | copy-start | bytes 1156
  10.4 5.0 %copy-start.32 = (bf16[192]{0:T(256)(128)(2,1)S(1)}, bf16[192]{0:T(256)(128)(2,1)}, u32[]{:S(2)}) copy-start(bf16[192]{0:T(256)(128)(2,1)} %param.20) | copy-start | bytes 1156
  10.4 5.2 %copy-start.33 = (bf16[192]{0:T(256)(128)(2,1)S(1)}, bf16[192]{0:T(256)(128)(2,1)}, u32[]{:S(2)}) copy-start(bf16[192]{0:T(256)(128)(2,1)} %param.22) | copy-start | bytes 1156
  10.4 5.5 %copy-start.34 = (bf16[192]{0:T(256)(128)(2,1)S(1)}, bf16[192]{0:T(256)(128)(2,1)}, u32[]{:S(2)}) copy-start(bf16[192]{0:T(256)(128)(2,1)} %param.23) | copy-start | bytes 1156
  10.4 5.7 %copy-start.35 = (bf16[192]{0:T(256)(128)(2,1)S(1)}, bf16[192]{0:T(256)(128)(2,1)}, u32[]{:S(2)}) copy-start(bf16[192]{0:T(256)(128)(2,1)} %param.24) | copy-start | bytes 1156
  12.3 32.1 %copy-start.19 = (f32[1576]{0:T(1024)}, f32[1576]{0:T(1024)S(1)}, u32[]{:S(2)}) copy-start(f32[1576]{0:T(1024)S(1)} %div.27) | copy-start | bytes 18916
  13.2 31.2 %copy-start.21 = (f32[1576]{0:T(1024)}, f32[1576]{0:T(1024)S(1)}, u32[]{:S(2)}) copy-start(f32[1576]{0:T(1024)S(1)} %rsqrt.21) | copy-start | bytes 18916
  22.3 91.6 %copy-start.23 = (f32[384]{0:T(512)}, f32[384]{0:T(512)S(1)}, u32[]{:S(2)}) copy-start(f32[384]{0:T(512)S(1)} %convert_element_type.205) | copy-start | bytes 4612
  22.3 2.1 copy-start.15
  24.4 25.1 %copy-start.4 = (f32[1576,384]{1,0:T(8,128)}, f32[1576,384]{1,0:T(8,128)S(1)}, u32[]{:S(2)}) copy-start(f32[1576,384]{1,0:T(8,128)S(1)} %reshape.179) | copy-start | bytes 7262212
  44.4 0.9 copy-start.13
  71.4 5.6 %copy-start.9 = (bf16[8,197,1,6,64]{1,4,3,0,2:T(8,128)(2,1)}, bf16[8,197,1,6,64]{1,4,3,0,2:T(8,128)(2,1)S(1)}, u32[]{:S(2)}) copy-start(bf16[8,197,1,6,64]{1,4,3,0,2:T(8,128)(2,1)S(1)} %copy.114) | copy-start | bytes 3631108
  75.5 1.5 copy-start.1
  77.0 3.8 copy-start
  84.3 6.3 %copy-start.7 = (bf16[8,197,1,6,64]{1,4,3,0,2:T(8,128)(2,1)}, bf16[8,197,1,6,64]{1,4,3,0,2:T(8,128)(2,1)S(1)}, u32[]{:S(2)}) copy-start(bf16[8,197,1,6,64]{1,4,3,0,2:T(8,128)(2,1)S(1)} %copy.113) | copy-start | bytes 3631108
  91.6 2.6 copy-start.17
  103.6 51.0 %copy-start.2 = (f32[1576,384]{1,0:T(8,128)}, f32[1576,384]{1,0:T(8,128)S(1)}, u32[]{:S(2)}) copy-start(f32[1576,384]{1,0:T(8,128)S(1)} %get-tuple-element.127) | copy-start | bytes 7262212
  103.6 0.7 copy-start.26
  146.0 8.6 %copy-start.28 = (bf16[384,1536]{1,0:T(8,128)(2,1)S(1)}, bf16[384,1536]{1,0:T(8,128)(2,1)}, u32[]{:S(2)}) copy-start(bf16[384,1536]{1,0:T(8,128)(2,1)} %all-gather.4.cloned.1.call-done) | copy-start | bytes 3538948
  154.6 3.3 copy-start.37
  154.6 3.3 copy-start.12
  158.0 3.3 copy-start.11
  197.2 5.2 %copy-start.10 = (bf16[8,197,1,6,64]{1,4,3,0,2:T(8,128)(2,1)S(1)}, bf16[8,197,1,6,64]{1,4,3,0,2:T(8,128)(2,1)}, u32[]{:S(2)}) copy-start(bf16[8,197,1,6,64]{1,4,3,0,2:T(8,128)(2,1)} %copy-done.9) | copy-start | bytes 3631108
  197.2 10.7 %slice-start = ((s8[9830400]{0:T(1024)(128)(4,1)}), s8[4194304]{0:T(1024)(128)(4,1)S(1)}, s32[]{:S(2)}) async-start(s8[9830400]{0:T(1024)(128)(4,1)} %bitcast.70), calls=%async_computation.11 | async-start | bytes 8388608
  197.2 10.7 %slice-start.1 = ((s8[9830400]{0:T(1024)(128)(4,1)}), s8[4194304]{0:T(1024)(128)(4,1)S(1)}, s32[]{:S(2)}) async-start(s8[9830400]{0:T(1024)(128)(4,1)} %bitcast.70), calls=%async_computation.12 | async-start | bytes 8388608
  202.4 5.4 %slice-start.2 = ((s8[9830400]{0:T(1024)(128)(4,1)}), s8[1441792]{0:T(1024)(128)(4,1)S(1)}, s32[]{:S(2)}) async-start(s8[9830400]{0:T(1024)(128)(4,1)} %bitcast.70), calls=%async_computation.13 | async-start | bytes 2883584
  202.4 5.4 %copy-start.8 = (bf16[8,197,6,64]{1,3,2,0:T(8,128)(2,1)S(1)}, bf16[8,197,6,64]{1,3,2,0:T(8,128)(2,1)}, u32[]{:S(2)}) copy-start(bf16[8,197,6,64]{1,3,2,0:T(8,128)(2,1)} %copy.95) | copy-start | bytes 3631108
  211.0 48.6 %reduce-scatter.5.cloned.1.call-start = ((), (), s32[]{:S(2)}) async-start(), calls=%async_computation.6 | async-start | bytes 1327104 | tf_op jit(solution)/shard_map/reduce_scatter | solution.py:207
  233.9 43.2 %reduce-scatter.9.cloned.1.call-start = ((), (), s32[]{:S(2)}) async-start(), calls=%async_computation.8 | async-start | bytes 1769472 | tf_op jit(solution)/shard_map/reduce_scatter | solution.py:228
  240.6 61.0 %reduce-scatter.11.cloned.1.call-start = ((), (), s32[]{:S(2)}) async-start(), calls=%async_computation.9 | async-start | bytes 1769472 | tf_op jit(solution)/shard_map/reduce_scatter | solution.py:234
  240.6 9.8 %copy-start.36 = (bf16[192]{0:T(256)(128)(2,1)S(1)}, bf16[192]{0:T(256)(128)(2,1)}, u32[]{:S(2)}) copy-start(bf16[192]{0:T(256)(128)(2,1)} %param.28) | copy-start | bytes 1156
  240.6 10.3 %copy-start.14 = (bf16[384,1152]{1,0:T(8,128)(2,1)S(1)}, bf16[384,1152]{1,0:T(8,128)(2,1)}, u32[]{:S(2)}) copy-start(bf16[384,1152]{1,0:T(8,128)(2,1)} %copy-done.13) | copy-start | bytes 2654212
  240.7 10.2 %copy-start.20 = (f32[1576]{0:T(1024)S(1)}, f32[1576]{0:T(1024)}, u32[]{:S(2)}) copy-start(f32[1576]{0:T(1024)} %copy-done.19) | copy-start | bytes 18916
  240.7 10.2 %copy-start.22 = (f32[1576]{0:T(1024)S(1)}, f32[1576]{0:T(1024)}, u32[]{:S(2)}) copy-start(f32[1576]{0:T(1024)} %copy-done.21) | copy-start | bytes 18916
  240.7 10.2 %copy-start.24 = (f32[384]{0:T(512)S(1)}, f32[384]{0:T(512)}, u32[]{:S(2)}) copy-start(f32[384]{0:T(512)} %copy-done.23) | copy-start | bytes 4612
  247.5 155.3 %all-reduce.23.cloned.1.call-start = ((), (), s32[]{:S(2)}) async-start(), calls=%async_computation.10 | async-start | bytes 3538944 | tf_op jit(solution)/shard_map/psum | solution.py:244
  250.9 6.5 %copy-start.5 = (f32[1576,384]{1,0:T(8,128)S(1)}, f32[1576,384]{1,0:T(8,128)}, u32[]{:S(2)}) copy-start(f32[1576,384]{1,0:T(8,128)} %copy-done.4) | copy-start | bytes 7262212
  347.0 5.5 %copy-start.3 = (f32[1576,384]{1,0:T(8,128)S(1)}, f32[1576,384]{1,0:T(8,128)}, u32[]{:S(2)}) copy-start(f32[1576,384]{1,0:T(8,128)} %copy-done.2) | copy-start | bytes 7262212
  349.9 2.6 copy-start.27
  402.8 4.4 %copy-start.16 = (bf16[192,1152]{1,0:T(8,128)(2,1)S(1)}, bf16[192,1152]{1,0:T(8,128)(2,1)}, u32[]{:S(2)}) copy-start(bf16[192,1152]{1,0:T(8,128)(2,1)} %get-tuple-element.92) | copy-start | bytes 1327108
  402.8 5.4 %copy-start.18 = (bf16[192,384]{1,0:T(8,128)(2,1)S(1)}, bf16[192,384]{1,0:T(8,128)(2,1)}, u32[]{:S(2)}) copy-start(bf16[192,384]{1,0:T(8,128)(2,1)} %get-tuple-element.93) | copy-start | bytes 442372
Sparse Core Ops, SparseCore 0:
  9.6 32.8 all-gather.3
  44.0 22.3 all-gather.5
  211.1 12.0 reduce-scatter.6
  234.0 18.5 reduce-scatter.4
  255.3 21.7 reduce-scatter.8
  279.8 21.7 reduce-scatter.10
  305.5 97.2 all-reduce.22
where the time goes:
time: 421 us; the launch traced here: 416 us
  matrix products  113 us (27%)
  local copies, waits for them, and re-layouts  85.2 us (20%)
  waiting for transfers between devices  84.9 us (20%)
  blocking collectives  75.7 us (18%)
  other arithmetic  39.7 us (9%)
  between operations  17 us (4%)
    psum x1, waiting for transfers between devices, per_device(): lax.psum(owned[2].astype(jnp.bfloat16), 'rep').astype(jnp.float32)  41.4 us
    dot_general x4, matrix products, product(): return jnp.dot(left, right, preferred_element_type=jnp.float32)  39.9 us
    psum x1, blocking collectives, per_device(): lax.psum(owned[0].astype(jnp.bfloat16), 'rep').astype(jnp.float32)  32.4 us
    reduce_scatter x1, waiting for transfers between devices, per_device(): lax.psum_scatter(grad_drop_weight.astype(jnp.bfloat16), 'fsdp', scatter_d...  24.5 us
    unnamed x116, local copies, waits for them, and re-layouts  23.6 us
    dot_general x4, matrix products, product_left(): lax.dot_general(left, right, (((0,), (0,)), ((), ())), preferred_element_...  20.4 us
    dot_general x4, matrix products, product_right(): lax.dot_general(left, right, (((1,), (1,)), ((), ())), preferred_element_...  20.3 us
    all_gather x1, blocking collectives, per_device(): lax.all_gather(qkv_weight, 'fsdp', axis=0, tiled=True)  20 us
  transfers between devices with their start and end apart: 7, of which 3 were waited for; matrix products, arithmetic and copies ran while one was open for 39% of the time, Pallas kernels for 0%

commit v1 on v0

--- a/solution.py
+++ b/solution.py
@@ -8,6 +8,18 @@
 epsilon = 1e-06
 root_half = 0.7071067811865476
 gauss_norm = 0.3989422804014327
+
+
+def collect(x, axis, dim):
+    ways, here, lap = (lax.axis_size(axis), lax.axis_index(axis), x.shape[dim])
+    line, have = (x, 1)
+    while have < ways:
+        line = jnp.concatenate(
+            [line, lax.ppermute(line, axis, [(d, (d - have) % ways) for d in range(ways)])],
+            axis=dim,
+        )
+        have = 2 * have
+    return jnp.roll(line, here * lap, axis=dim)
 
 
 def norm_forward(inputs, gain_vec, shift_vec):
@@ -75,7 +87,7 @@
     gathered = (
         lax.all_gather(gain_one, "fsdp", axis=0, tiled=True),
         lax.all_gather(shift_one, "fsdp", axis=0, tiled=True),
-        lax.all_gather(qkv_weight, "fsdp", axis=0, tiled=True),
+        collect(qkv_weight, "fsdp", 0),
         lax.all_gather(query_bias, "fsdp", axis=0, tiled=True),
         lax.all_gather(value_bias, "fsdp", axis=0, tiled=True),
         lax.all_gather(out_weight, "fsdp", axis=0, tiled=True),

time: 421 us -> 407 us (0.967)
  waiting for transfers between devices: 84.9 us -> 74.6 us
  blocking collectives: 75.7 us -> 65.5 us
    reduce_scatter x1, waiting for transfers between devices: 17.5 us -> 7.81 us  [per_device(): lax.psum_scatter(grad_lift_weight.astype(jnp.bfloat16), 'fsdp', scatter_d...]
    all_gather x1, blocking collectives: 20 us -> 11 us  [per_device(): lax.all_gather(qkv_weight, 'fsdp', axis=0, tiled=True)]
    unnamed x116 -> x114, local copies, waits for them, and re-layouts: 23.6 us -> 22.3 us
  transfers between devices with their start and end apart: 7 -> 8, of which waited for: 3 -> 3; matrix products, arithmetic and copies ran while one was open for 39% -> 42% of each run, Pallas kernels for 0% -> 0%
where the time goes in v1:
time: 407 us; the launch traced here: 401 us
  matrix products  116 us (29%)
  local copies, waits for them, and re-layouts  83.8 us (21%)
  waiting for transfers between devices  74.6 us (18%)
  blocking collectives  65.5 us (16%)
  other arithmetic  40 us (10%)
  between operations  17.3 us (4%)
    dot_general x4, matrix products, product(): return jnp.dot(left, right, preferred_element_type=jnp.float32)  42.8 us
    psum x1, waiting for transfers between devices, per_device(): lax.psum(owned[2].astype(jnp.bfloat16), 'rep').astype(jnp.float32)  41.4 us
    psum x1, blocking collectives, per_device(): lax.psum(owned[0].astype(jnp.bfloat16), 'rep').astype(jnp.float32)  32.4 us
    reduce_scatter x1, waiting for transfers between devices, per_device(): lax.psum_scatter(grad_drop_weight.astype(jnp.bfloat16), 'fsdp', scatter_d...  24.6 us
    unnamed x114, local copies, waits for them, and re-layouts  22.3 us
    dot_general x4, matrix products, product_right(): lax.dot_general(left, right, (((1,), (1,)), ((), ())), preferred_element_...  20.6 us
    dot_general x4, matrix products, product_left(): lax.dot_general(left, right, (((0,), (0,)), ((), ())), preferred_element_...  20.3 us
    convert_element_type x2, local copies, waits for them, and re-layouts, per_device(): d_projected = jnp.stack([d_query, d_key, d_value], axis=2).reshape(tok_ro...  14.3 us
  transfers between devices with their start and end apart: 8, of which 3 were waited for; matrix products, arithmetic and copies ran while one was open for 42% of the time, Pallas kernels for 0%

profile of v1, /device:TPU:0, one launch (start us, length us, event | category | flops | bytes accessed | tf_op | source)
XLA Modules:
  0.0 400.8 jit_solution(16456336239138708433)
XLA Ops:
  8.0 3.0 collective-permute-start
  18.7 5.0 %all-reduce.20 = (bf16[384]{0:T(512)(128)(2,1)S(1)}, bf16[384]{0:T(512)(128)(2,1)S(1)}, bf16[384]{0:T(512)(128)(2,1)S(1)}, bf16[384]{0:T(512)(128)(2,1)S(1)}, bf...) all-reduce(bf16[384]{0:T(512)(128)(2,1)S(1)} %dynamic-update-slice., ...), channel_id=1, replica_groups=mesh['rep'=16,'fsdp'=2] {'fsdp'}, use_global_device_ids=true, to_apply=%add.3 | all-reduce | flops 2688 | bytes 10752
  25.8 4.4 %all-gather = bf16[2,1,768]{2,1,0:T(2,128)(2,1)S(1)} all-gather(bf16[1,1,768]{2,1,0:T(2,128)(2,1)S(1)} %reshape.209), channel_id=1, replica_groups=mesh['rep'=16,'fsdp'=2] {'fsdp'}, dimensions={0}, use_global_device_ids=true | all-gather | bytes 4608 | tf_op jit(solution)/shard_map/all_gather | solution.py:98
  30.2 2.5 copy.93
  32.7 2.7 reshape.182
  38.4 2.7 convert_element_type.235
  41.1 5.8 %all_gather.48 = bf16[384,384]{1,0:T(8,128)(2,1)S(1)} all-gather(bf16[192,384]{1,0:T(8,128)(2,1)S(1)} %copy-done.16), channel_id=1, replica_groups=mesh['rep'=16,'fsdp'=2] {'fsdp'}, dimensions={0}, use_global_device_ids=true | all-gather | bytes 442368 | tf_op jit(solution)/shard_map/all_gather | solution.py:93
  47.0 6.9 %fusion.16 = bf16[1576,1152]{1,0:T(8,128)(2,1)} fusion(f32[1152]{0:T(1024)S(1)} %maximum_convert_fusion.1, f32[1576,384]{1,0:T(8,128)S(1)} %reshape.179, f32[384]{0:T(512)S(1)} %convert_element_type.206, f32[384]{0:T(512)S(1)} %convert_element_type.205, f32[1576]{0:T(1024)S(1)} %rsqrt.21, f32[1576]{0:T(1024)S(1)} %div.27, s32[]{:T(128)S(6)} %select_n.14, ...), kind=kOutput, calls=%fused_computation.34 | convolution fusion | flops 1404539904 | bytes 6956868 | tf_op jit(solution)/shard_map/dot_general | solution.py:47
  53.9 11.7 %reshape.237 = bf16[8,197,3,6,64]{4,3,2,1,0:T(8,128)(2,1)} reshape(bf16[1576,1152]{1,0:T(8,128)(2,1)} %fusion.16) | data formatting | bytes 7262208 | tf_op jit(solution)/shard_map/reshape | solution.py:129
  65.6 6.7 %fusion.49 = (bf16[8,197,1,6,64]{4,3,2,1,0:T(8,128)(2,1)}, bf16[8,197,1,6,64]{4,3,2,1,0:T(8,128)(2,1)}, bf16[8,197,1,6,64]{4,3,2,1,0:T(8,128)(2,1)}) fusion(bf16[8,197,3,6,64]{4,3,2,1,0:T(8,128)(2,1)} %reshape.237), kind=kLoop, calls=%fused_computation.105 | loop fusion | bytes 7262208 | tf_op jit(solution)/shard_map/slice | solution.py:130
  72.3 3.5 copy.114
  75.8 4.0 %copy.115 = bf16[8,197,1,6,64]{1,4,3,0,2:T(8,128)(2,1)S(1)} copy(bf16[8,197,1,6,64]{4,3,2,1,0:T(8,128)(2,1)} %get-tuple-element.119) | data formatting | bytes 2420736
  81.4 2.0 exponential_reduce_fusion
  85.2 3.5 copy.113
  88.7 6.3 %fusion.29 = bf16[8,197,6,64]{1,3,2,0:T(8,128)(2,1)S(1)} fusion(bf16[8,197,1,6,64]{1,4,3,0,2:T(8,128)(2,1)S(1)} %copy.113, f32[8,6,197,197]{2,3,1,0:T(8,128)} %copy-done, f32[8,6,197]{2,1,0:T(8,128)S(1)} %log_add_fusion), kind=kOutput, calls=%fused_computation.77 | convolution fusion | flops 244636176 | bytes 9909888 | tf_op jit(solution)/shard_map/ihqk,ikhe->iqhe/dot_general | solution.py:138
  96.0 3.0 convert_element_type.213
  99.0 3.2 fusion.52
  102.8 26.6 %fusion.2 = (bf16[1576,1536]{1,0:T(8,128)(2,1)}, f32[1576,1536]{1,0:T(8,128)}) fusion(f32[1536]{0:T(1024)S(1)} %reshape.211, bf16[384,1536]{1,0:T(8,128)(2,1)} %all-gather.4.cloned.1.call-done, f32[1576,384]{1,0:T(8,128)S(1)} %get-tuple-element.127, f32[384]{0:T(512)S(1)} %convert_element_type.216, f32[384]{0:T(512)S(1)} %convert_element_type.215, ...), kind=kOutput, calls=%fused_computation.9 | convolution fusion | flops 2021919744 | bytes 18146624 | tf_op jit(solution)/shard_map/dot_general | solution.py:47
  129.4 8.6 %fusion.53 = (bf16[1536]{0:T(1024)(128)(2,1)S(1)}, bf16[1576,1536]{1,0:T(8,128)(2,1)S(1)}) fusion(f32[1576,1536]{1,0:T(8,128)} %get-tuple-element.129, bf16[1576,384]{1,0:T(8,128)(2,1)} %reshape.182, bf16[1536,384]{1,0:T(8,128)(2,1)} %all-gather.6.cloned.1.call-done), kind=kOutput, calls=%fused_computation.109 | convolution fusion | flops 1885751808 | bytes 16917504 | tf_op jit(solution)/shard_map/dot_general | solution.py:57
  138.0 3.3 multiply_reduce_fusion.2
  141.3 3.4 convert_reduce_fusion.2
  146.3 2.0 convolution_convert_fusion.3
  148.4 4.8 %reshape.238 = bf16[8,197,6,64]{3,2,1,0:T(8,128)(2,1)} reshape(bf16[1576,384]{1,0:T(8,128)(2,1)} %convolution_convert_fusion.3) | data formatting | bytes 2420736 | tf_op jit(solution)/shard_map/reshape | solution.py:182
  153.1 4.6 %copy.95 = bf16[8,197,6,64]{1,3,2,0:T(8,128)(2,1)} copy(bf16[8,197,6,64]{3,2,1,0:T(8,128)(2,1)} %reshape.238) | data formatting | bytes 2420736 | tf_op jit(solution)/shard_map/reshape | solution.py:182
  157.7 11.1 %multiply_reduce_fusion = (f32[8,6,197]{2,1,0:T(8,128)S(1)}, f32[8,6,197,197]{2,3,1,0:T(8,128)}) fusion(f32[8,6,197,197]{2,3,1,0:T(8,128)} %copy-done, f32[8,6,197]{2,1,0:T(8,128)S(1)} %log_add_fusion, bf16[8,197,6,64]{1,3,2,0:T(8,128)(2,1)} %copy.95, bf16[8,197,1,6,64]{1,4,3,0,2:T(8,128)(2,1)} %copy-done.7), kind=kOutput, calls=%fused_computation.3 | convolution fusion | flops 245884368 | bytes 17399040 | tf_op jit(solution)/shard_map/iqhe,ikhe->ihqk/dot_general | solution.py:187
  168.8 11.5 %multiply_convert_fusion = bf16[8,6,197,197]{2,3,1,0:T(8,128)(2,1)} fusion(f32[8,6,197,197]{2,3,1,0:T(8,128)} %get-tuple-element.132, f32[8,6,197,197]{2,3,1,0:T(8,128)} %copy-done, f32[8,6,197]{2,1,0:T(8,128)S(1)} %get-tuple-element.131, f32[8,6,197]{2,1,0:T(8,128)S(1)} %log_add_fusion), kind=kLoop, calls=%fused_computation.2 | loop fusion | flops 9314160 | bytes 18703968 | tf_op jit(solution)/shard_map/convert_element_type | solution.py:189
  180.3 5.2 %multiply_bitcast_fusion.1 = bf16[8,197,1,6,64]{1,4,3,0,2:T(8,128)(2,1)} fusion(bf16[8,6,197,197]{2,3,1,0:T(8,128)(2,1)} %multiply_convert_fusion, bf16[8,197,1,6,64]{1,4,3,0,2:T(8,128)(2,1)} %copy-done.1), kind=kOutput, calls=%fused_computation.37 | convolution fusion | flops 239652864 | bytes 6146400 | tf_op jit(solution)/shard_map/ihqk,ikhe->iqhe/dot_general | solution.py:191
  185.5 5.4 %multiply_bitcast_fusion = bf16[8,197,1,6,64]{1,4,3,0,2:T(8,128)(2,1)} fusion(bf16[8,6,197,197]{2,3,1,0:T(8,128)(2,1)} %multiply_convert_fusion, bf16[8,197,1,6,64]{1,4,3,0,2:T(8,128)(2,1)S(1)} %copy-done.10), kind=kOutput, calls=%fused_computation.36 | convolution fusion | flops 239652864 | bytes 6146400 | tf_op jit(solution)/shard_map/ihqk,iqhe->ikhe/dot_general | solution.py:195
  191.0 3.1 convolution_bitcast_fusion
  194.1 3.2 fusion.48
  197.4 5.5 %copy.100 = bf16[8,197,3,6,64]{1,0,4,3,2:T(8,128)(2,1)} copy(bf16[8,197,3,6,64]{1,4,3,0,2:T(8,128)(2,1)S(1)} %get-tuple-element.116) | data formatting | bytes 7262208 | tf_op jit(solution)/shard_map/convert_element_type | solution.py:201
  202.8 8.9 %convert_element_type.228 = bf16[1576,1152]{0,1:T(8,128)(2,1)} reshape(bf16[8,197,3,6,64]{1,0,4,3,2:T(8,128)(2,1)} %copy.100) | data formatting | bytes 7262208 | tf_op jit(solution)/shard_map/convert_element_type | solution.py:201
  211.7 5.3 %convolution_convert_fusion = bf16[384,1152]{1,0:T(8,128)(2,1)} fusion(bf16[1576,384]{1,0:T(8,128)(2,1)} %convert_element_type.235, bf16[1576,1152]{0,1:T(8,128)(2,1)} %convert_element_type.228), kind=kOutput, calls=%fused_computation.42 | convolution fusion | flops 1394786304 | bytes 5726208 | tf_op jit(solution)/shard_map/dot_general | solution.py:51
  217.1 6.6 %convolution_convert_fusion.2 = bf16[384,1536]{1,0:T(8,128)(2,1)} fusion(bf16[1576,1536]{1,0:T(8,128)(2,1)} %copy-done.36, f32[1576,384]{1,0:T(8,128)} %copy-done.2, f32[384]{0:T(512)S(1)} %convert_element_type.216, f32[384]{0:T(512)S(1)} %convert_element_type.215, f32[1576]{0:T(1024)S(1)} %add_rsqrt_fusion, f32[1576]{0:T(1024)S(1)} %broadcast_multiply_fusion.4), kind=kOutput, calls=%fused_computation.45 | convolution fusion | flops 1862740992 | bytes 8457536 | tf_op jit(solution)/shard_map/dot_general | solution.py:51
  223.8 6.7 %convolution_convert_fusion.1 = bf16[1536,384]{1,0:T(8,128)(2,1)} fusion(bf16[1576,1536]{1,0:T(8,128)(2,1)} %get-tuple-element.128, bf16[1576,384]{1,0:T(8,128)(2,1)} %reshape.182), kind=kOutput, calls=%fused_computation.44 | convolution fusion | flops 1859715072 | bytes 7231488 | tf_op jit(solution)/shard_map/dot_general | solution.py:51
  233.8 11.0 %all_gather.56 = bf16[384,1152]{1,0:T(8,128)(2,1)S(1)} all-gather(bf16[192,1152]{1,0:T(8,128)(2,1)S(1)} %copy-done.14), channel_id=1, replica_groups=mesh['rep'=16,'fsdp'=2] {'fsdp'}, dimensions={0}, use_global_device_ids=true | all-gather | bytes 1327104 | tf_op jit(solution)/shard_map/all_gather | solution.py:153
  244.8 6.7 %multiply_reduce_fusion.3 = (bf16[384]{0:T(512)(128)(2,1)S(1)}, f32[1576]{0:T(1024)S(1)}, f32[1576]{0:T(1024)S(1)}, bf16[384]{0:T(512)(128)(2,1)S(1)}, f32[1576,384]{1,0:T(8,128)S(1)}) fusion(f32[1576,384]{1,0:T(8,128)} %copy-done.4, f32[1576]{0:T(1024)S(1)} %copy-done.21, f32[1576]{0:T(1024)S(1)} %copy-done.19, f32[384]{0:T(512)S(1)} %copy-done.23, ...), kind=kOutput, calls=%fused_computation.49 | convolution fusion | flops 1399786752 | bytes 9385600 | tf_op jit(solution)/shard_map/dot_general | solution.py:57
  251.6 2.2 add_convert_fusion.1
  253.8 7.8 %reduce-scatter.9.cloned.1.call-done = bf16[192,1536]{1,0:T(8,128)(2,1)} async-done(((bf16[384,1536]{1,0:T(8,128)(2,1)}), bf16[192,1536]{1,0:T(8,128)(2,1)}) %reduce-scatter.9.cloned.1.call-update) | async-done | bytes 589840 | tf_op jit(solution)/shard_map/reduce_scatter | solution.py:240
  261.6 24.6 %reduce-scatter.11.cloned.1.call-done = bf16[768,384]{1,0:T(8,128)(2,1)} async-done(((bf16[1536,384]{1,0:T(8,128)(2,1)}), bf16[768,384]{1,0:T(8,128)(2,1)}) %reduce-scatter.11.cloned.1.call-update) | async-done | bytes 589840 | tf_op jit(solution)/shard_map/reduce_scatter | solution.py:246
  286.4 7.0 %all-reduce.19 = (bf16[384]{0:T(512)(128)(2,1)S(1)}, bf16[384]{0:T(512)(128)(2,1)S(1)}, bf16[384]{0:T(512)(128)(2,1)S(1)}, bf16[384]{0:T(512)(128)(2,1)S(1)}, bf...) all-reduce(bf16[384]{0:T(512)(128)(2,1)S(1)} %dynamic-update-slice., ...), channel_id=1, replica_groups=mesh['rep'=16,'fsdp'=2] {'fsdp'}, use_global_device_ids=true, to_apply=%add.7 | all-reduce | flops 4992 | bytes 19968
  294.0 32.4 %all-reduce.17 = (bf16[192]{0:T(256)(128)(2,1)S(1)}, bf16[192]{0:T(256)(128)(2,1)S(1)}, bf16[192]{0:T(256)(128)(2,1)S(1)}, bf16[192]{0:T(256)(128)(2,1)S(1)}, bf...) all-reduce(bf16[192]{0:T(256)(128)(2,1)S(1)} %dynamic-slice.9, ...), channel_id=1, replica_groups=mesh['rep'=16,'fsdp'=2] {'rep'}, use_global_device_ids=true, to_apply=%region_13.14 | all-reduce | flops 2304 | bytes 9216 | tf_op jit(solution)/shard_map/psum | solution.py:254
  331.5 2.9 reshape.184
  334.4 2.6 copy.104
  337.0 6.1 %fusion.20 = bf16[1576,384]{1,0:T(8,128)(2,1)} fusion(f32[1576,384]{1,0:T(8,128)S(1)} %copy-done.3, bf16[1576,1536]{1,0:T(8,128)(2,1)} %get-tuple-element.128, bf16[1536,384]{1,0:T(8,128)(2,1)S(1)} %copy-done.26, f32[384]{0:T(512)S(1)} %convert_element_type.220), kind=kOutput, calls=%fused_computation.43 | convolution fusion | flops 1860940800 | bytes 9653760 | tf_op jit(solution)/shard_map/dot_general | solution.py:47
  345.9 41.4 %all-reduce.23.cloned.1.call-done = (bf16[192,1152]{1,0:T(8,128)(2,1)}, bf16[192,384]{1,0:T(8,128)(2,1)}, bf16[192,1536]{1,0:T(8,128)(2,1)}, bf16[768,384]{1,0:T(8,128)(2,1)}) async-done(((bf16[192,1152]{1,0:T(8,128)(2,1)}, bf16[192,384]{1,0:T(8,128)(2,1)}, bf16[192,1536]{1,0:T(8,128)(2,1)}, bf16[768,384]{1,0:T(8,128)(2,1)}), (bf16[192,1152]{1,0:T(8,128)(2,1)}, bf16[192,384]{1,0:T(8,128)(2,1)}, ...) | async-done | bytes 1769488 | tf_op jit(solution)/shard_map/psum | solution.py:256
  387.3 2.3 convert_element_type.251
  389.6 2.2 convert_element_type.254
  (178 shorter events, 31.9 us)
Async XLA Ops:
  7.2 5.5 %copy-start.6 = (bf16[8,197,384]{2,0,1:T(8,128)(2,1)S(1)}, bf16[8,197,384]{2,0,1:T(8,128)(2,1)}, u32[]{:S(2)}) copy-start(bf16[8,197,384]{2,0,1:T(8,128)(2,1)} %param.15) | copy-start | bytes 3631108
  7.2 95.6 %all-gather.4.cloned.1.call-start = ((), (), s32[]{:S(2)}) async-start(), calls=%async_computation.4 | async-start | bytes 1769472 | tf_op jit(solution)/shard_map/all_gather | solution.py:97
  7.9 121.4 %all-gather.6.cloned.1.call-start = ((), (), s32[]{:S(2)}) async-start(), calls=%async_computation.5 | async-start | bytes 1769472 | tf_op jit(solution)/shard_map/all_gather | solution.py:99
  8.0 39.0 %collective-permute-start = (bf16[192,1152]{1,0:T(8,128)(2,1)}, bf16[192,1152]{1,0:T(8,128)(2,1)}, u32[]{:S(2)}, u32[]{:S(2)}) collective-permute-start(bf16[192,1152]{1,0:T(8,128)(2,1)} %param.18), channel_id=1, source_target_pairs={{0,1},{1,0},{2,3},{3,2},{4,5},{5,4},{6,7},{7,6},{8,9},{9,8},{10,11... | collective-permute-start | bytes 1327112 | tf_op jit(solution)/shard_map/ppermute | solution.py:18
  11.0 242.8 %reduce-scatter.7.cloned.1.call-start = ((), (), s32[]{:S(2)}) async-start(), calls=%async_computation.7 | async-start | bytes 442368 | tf_op jit(solution)/shard_map/reduce_scatter | solution.py:228
  12.7 3.0 copy-start.24
  12.7 4.3 %copy-start.28 = (bf16[192]{0:T(256)(128)(2,1)S(1)}, bf16[192]{0:T(256)(128)(2,1)}, u32[]{:S(2)}) copy-start(bf16[192]{0:T(256)(128)(2,1)} %param.16) | copy-start | bytes 1156
  12.7 4.5 %copy-start.29 = (bf16[192]{0:T(256)(128)(2,1)S(1)}, bf16[192]{0:T(256)(128)(2,1)}, u32[]{:S(2)}) copy-start(bf16[192]{0:T(256)(128)(2,1)} %param.17) | copy-start | bytes 1156
  12.7 4.8 %copy-start.30 = (bf16[192]{0:T(256)(128)(2,1)S(1)}, bf16[192]{0:T(256)(128)(2,1)}, u32[]{:S(2)}) copy-start(bf16[192]{0:T(256)(128)(2,1)} %param.19) | copy-start | bytes 1156
  12.7 5.0 %copy-start.31 = (bf16[192]{0:T(256)(128)(2,1)S(1)}, bf16[192]{0:T(256)(128)(2,1)}, u32[]{:S(2)}) copy-start(bf16[192]{0:T(256)(128)(2,1)} %param.20) | copy-start | bytes 1156
  12.7 5.3 %copy-start.32 = (bf16[192]{0:T(256)(128)(2,1)S(1)}, bf16[192]{0:T(256)(128)(2,1)}, u32[]{:S(2)}) copy-start(bf16[192]{0:T(256)(128)(2,1)} %param.22) | copy-start | bytes 1156
  12.7 5.5 %copy-start.33 = (bf16[192]{0:T(256)(128)(2,1)S(1)}, bf16[192]{0:T(256)(128)(2,1)}, u32[]{:S(2)}) copy-start(bf16[192]{0:T(256)(128)(2,1)} %param.23) | copy-start | bytes 1156
  12.7 5.7 %copy-start.34 = (bf16[192]{0:T(256)(128)(2,1)S(1)}, bf16[192]{0:T(256)(128)(2,1)}, u32[]{:S(2)}) copy-start(bf16[192]{0:T(256)(128)(2,1)} %param.24) | copy-start | bytes 1156
  14.7 32.3 %copy-start.18 = (f32[1576]{0:T(1024)}, f32[1576]{0:T(1024)S(1)}, u32[]{:S(2)}) copy-start(f32[1576]{0:T(1024)S(1)} %div.27) | copy-start | bytes 18916
  15.6 31.4 %copy-start.20 = (f32[1576]{0:T(1024)}, f32[1576]{0:T(1024)S(1)}, u32[]{:S(2)}) copy-start(f32[1576]{0:T(1024)S(1)} %rsqrt.21) | copy-start | bytes 18916
  23.7 23.3 %copy-start.22 = (f32[384]{0:T(512)}, f32[384]{0:T(512)S(1)}, u32[]{:S(2)}) copy-start(f32[384]{0:T(512)S(1)} %convert_element_type.205) | copy-start | bytes 4612
  23.7 2.1 copy-start.25
  25.8 21.3 %copy-start.4 = (f32[1576,384]{1,0:T(8,128)}, f32[1576,384]{1,0:T(8,128)S(1)}, u32[]{:S(2)}) copy-start(f32[1576,384]{1,0:T(8,128)S(1)} %reshape.179) | copy-start | bytes 7262212
  37.2 3.9 copy-start.16
  37.2 9.8 %copy-start.13 = (bf16[192,1152]{1,0:T(8,128)(2,1)S(1)}, bf16[192,1152]{1,0:T(8,128)(2,1)}, u32[]{:S(2)}) copy-start(bf16[192,1152]{1,0:T(8,128)(2,1)} %param.18) | copy-start | bytes 1327108
  75.8 5.6 %copy-start.9 = (bf16[8,197,1,6,64]{1,4,3,0,2:T(8,128)(2,1)}, bf16[8,197,1,6,64]{1,4,3,0,2:T(8,128)(2,1)S(1)}, u32[]{:S(2)}) copy-start(bf16[8,197,1,6,64]{1,4,3,0,2:T(8,128)(2,1)S(1)} %copy.114) | copy-start | bytes 3631108
  79.8 1.6 copy-start.1
  81.4 3.8 copy-start
  88.7 6.3 %copy-start.7 = (bf16[8,197,1,6,64]{1,4,3,0,2:T(8,128)(2,1)}, bf16[8,197,1,6,64]{1,4,3,0,2:T(8,128)(2,1)S(1)}, u32[]{:S(2)}) copy-start(bf16[8,197,1,6,64]{1,4,3,0,2:T(8,128)(2,1)S(1)} %copy.113) | copy-start | bytes 3631108
  102.2 35.8 %copy-start.2 = (f32[1576,384]{1,0:T(8,128)}, f32[1576,384]{1,0:T(8,128)S(1)}, u32[]{:S(2)}) copy-start(f32[1576,384]{1,0:T(8,128)S(1)} %get-tuple-element.127) | copy-start | bytes 7262212
  129.4 8.6 %copy-start.27 = (bf16[384,1536]{1,0:T(8,128)(2,1)S(1)}, bf16[384,1536]{1,0:T(8,128)(2,1)}, u32[]{:S(2)}) copy-start(bf16[384,1536]{1,0:T(8,128)(2,1)} %all-gather.4.cloned.1.call-done) | copy-start | bytes 3538948
  138.0 3.3 copy-start.36
  138.0 3.3 copy-start.12
  141.3 3.4 copy-start.11
  180.3 5.2 %copy-start.10 = (bf16[8,197,1,6,64]{1,4,3,0,2:T(8,128)(2,1)S(1)}, bf16[8,197,1,6,64]{1,4,3,0,2:T(8,128)(2,1)}, u32[]{:S(2)}) copy-start(bf16[8,197,1,6,64]{1,4,3,0,2:T(8,128)(2,1)} %copy-done.9) | copy-start | bytes 3631108
  180.3 10.7 %slice-start = ((s8[9830400]{0:T(1024)(128)(4,1)}), s8[4194304]{0:T(1024)(128)(4,1)S(1)}, s32[]{:S(2)}) async-start(s8[9830400]{0:T(1024)(128)(4,1)} %bitcast.69), calls=%async_computation.11 | async-start | bytes 8388608
  180.3 10.7 %slice-start.1 = ((s8[9830400]{0:T(1024)(128)(4,1)}), s8[4194304]{0:T(1024)(128)(4,1)S(1)}, s32[]{:S(2)}) async-start(s8[9830400]{0:T(1024)(128)(4,1)} %bitcast.69), calls=%async_computation.12 | async-start | bytes 8388608
  185.5 5.4 %slice-start.2 = ((s8[9830400]{0:T(1024)(128)(4,1)}), s8[1441792]{0:T(1024)(128)(4,1)S(1)}, s32[]{:S(2)}) async-start(s8[9830400]{0:T(1024)(128)(4,1)} %bitcast.69), calls=%async_computation.13 | async-start | bytes 2883584
  185.5 5.4 %copy-start.8 = (bf16[8,197,6,64]{1,3,2,0:T(8,128)(2,1)S(1)}, bf16[8,197,6,64]{1,3,2,0:T(8,128)(2,1)}, u32[]{:S(2)}) copy-start(bf16[8,197,6,64]{1,3,2,0:T(8,128)(2,1)} %copy.95) | copy-start | bytes 3631108
  194.1 59.7 %reduce-scatter.5.cloned.1.call-start = ((), (), s32[]{:S(2)}) async-start(), calls=%async_computation.6 | async-start | bytes 1327104 | tf_op jit(solution)/shard_map/reduce_scatter | solution.py:219
  217.0 44.5 %reduce-scatter.9.cloned.1.call-start = ((), (), s32[]{:S(2)}) async-start(), calls=%async_computation.8 | async-start | bytes 1769472 | tf_op jit(solution)/shard_map/reduce_scatter | solution.py:240
  223.7 62.4 %reduce-scatter.11.cloned.1.call-start = ((), (), s32[]{:S(2)}) async-start(), calls=%async_computation.9 | async-start | bytes 1769472 | tf_op jit(solution)/shard_map/reduce_scatter | solution.py:246
  223.8 9.8 %copy-start.35 = (bf16[192]{0:T(256)(128)(2,1)S(1)}, bf16[192]{0:T(256)(128)(2,1)}, u32[]{:S(2)}) copy-start(bf16[192]{0:T(256)(128)(2,1)} %param.28) | copy-start | bytes 1156
  230.5 3.3 copy-start.14
  230.5 14.3 %copy-start.19 = (f32[1576]{0:T(1024)S(1)}, f32[1576]{0:T(1024)}, u32[]{:S(2)}) copy-start(f32[1576]{0:T(1024)} %copy-done.18) | copy-start | bytes 18916
  230.5 14.3 %copy-start.21 = (f32[1576]{0:T(1024)S(1)}, f32[1576]{0:T(1024)}, u32[]{:S(2)}) copy-start(f32[1576]{0:T(1024)} %copy-done.20) | copy-start | bytes 18916
  230.5 14.3 %copy-start.23 = (f32[384]{0:T(512)S(1)}, f32[384]{0:T(512)}, u32[]{:S(2)}) copy-start(f32[384]{0:T(512)} %copy-done.22) | copy-start | bytes 4612
  230.6 156.8 %all-reduce.23.cloned.1.call-start = ((), (), s32[]{:S(2)}) async-start(), calls=%async_computation.10 | async-start | bytes 3538944 | tf_op jit(solution)/shard_map/psum | solution.py:256
  244.8 6.8 %copy-start.5 = (f32[1576,384]{1,0:T(8,128)S(1)}, f32[1576,384]{1,0:T(8,128)}, u32[]{:S(2)}) copy-start(f32[1576,384]{1,0:T(8,128)} %copy-done.4) | copy-start | bytes 7262212
  331.5 5.5 %copy-start.3 = (f32[1576,384]{1,0:T(8,128)S(1)}, f32[1576,384]{1,0:T(8,128)}, u32[]{:S(2)}) copy-start(f32[1576,384]{1,0:T(8,128)} %copy-done.2) | copy-start | bytes 7262212
  334.4 2.6 copy-start.26
  387.3 4.4 %copy-start.15 = (bf16[192,1152]{1,0:T(8,128)(2,1)S(1)}, bf16[192,1152]{1,0:T(8,128)(2,1)}, u32[]{:S(2)}) copy-start(bf16[192,1152]{1,0:T(8,128)(2,1)} %get-tuple-element.92) | copy-start | bytes 1327108
  387.3 5.4 %copy-start.17 = (bf16[192,384]{1,0:T(8,128)(2,1)S(1)}, bf16[192,384]{1,0:T(8,128)(2,1)}, u32[]{:S(2)}) copy-start(bf16[192,384]{1,0:T(8,128)(2,1)} %get-tuple-element.93) | copy-start | bytes 442372
Sparse Core Ops, SparseCore 0:
  9.6 25.6 all-gather.3
  36.9 23.4 all-gather.5
  194.2 12.7 reduce-scatter.6
  217.2 20.0 reduce-scatter.4
  240.0 21.5 reduce-scatter.8
  264.3 21.7 reduce-scatter.10
  290.1 97.2 all-reduce.22
